TPU v7x, 128 devices: a whole 4x4x4 slice. The times are simulated.
128 devices in a mesh: row: 16 (over y, x), col: 8 (over z, core).
Axes of the slice: x: 4, y: 4, z: 4, core: 2. Of those that a mesh axis runs over, the one named last changes fastest.
Arguments:
- orbitals: float32 [32768, 1024], P('row', 'col'), may hold values from -6 to 6
- point_index: int32 [8192], replicated, may hold values from 0 to 32767, as said below
- coulomb: float32 [8192, 8192], P('row', 'col'), may hold values from -0.001953125 to 0.001953125
- fitting: float32 [32768, 8192], P('row', 'col'), may hold values from -0.0625 to 0.0625
Outputs:
- exchange_out: float32 [32768, 1024], P('row', 'col')
Inputs may be any that keep to these rules, and one draw needn't show every extreme that they name: `point_index`: indices are distinct. Grid index g lies in slab g // 2048. Of the 512 consecutive points of each row panel, at most 64 lie in one slab, and in every panel exactly 64 lie in one slab.
All inputs are finite; a program needn't handle non-finite values.
Results may differ from a plain program's by a relative error of at most 0.00012.
Values sent between devices are 32-bit elements; how exact they have to be, the bound alone decides.
No kernel may reach another device: no remote copies, remote signals or barrier semaphores. Data moves between devices by JAX's collectives and lax.ppermute only.
A program may use at most 64 MiB of HBM per device.

v0:
```python
import jax
import jax.numpy as jnp
from jax import lax
from jax.sharding import PartitionSpec as P


def per_device(orbitals, point_index, coulomb, fitting):
    row_count = lax.axis_size("row")
    slab_rows = orbitals.shape[0]
    band_cols = orbitals.shape[1]
    total_points = point_index.shape[0]
    per_panel = total_points // row_count
    slot_count = 2 * per_panel // row_count
    my_row = lax.axis_index("row")
    my_col = lax.axis_index("col")
    owner = point_index // slab_rows
    local_row = point_index - owner * slab_rows
    owner_grid = owner.reshape(row_count, per_panel)
    local_grid = local_row.reshape(row_count, per_panel)
    matches = (owner_grid[:, :, None] == jnp.arange(row_count)[None, None, :]).astype(jnp.int32)
    ranking = jnp.cumsum(matches, axis=1) - 1
    slot_grid = jnp.sum(jnp.where(matches > 0, ranking, 0), axis=2)
    mine = owner_grid == my_row
    chosen = mine[:, :, None] & (slot_grid[:, :, None] == jnp.arange(slot_count)[None, None, :])
    source_row = jnp.sum(jnp.where(chosen, local_grid[:, :, None], 0), axis=1)
    valid = jnp.any(chosen, axis=1)
    outgoing = jnp.where(valid[:, :, None], orbitals[source_row], 0.0)
    received = lax.all_to_all(outgoing, "row", split_axis=0, concat_axis=0, tiled=True)
    flattened = received.reshape(row_count * slot_count, band_cols)
    owner_mine = lax.dynamic_slice_in_dim(owner_grid, my_row, 1, 0)[0]
    slot_mine = lax.dynamic_slice_in_dim(slot_grid, my_row, 1, 0)[0]
    panel_strip = flattened[owner_mine * slot_count + slot_mine]
    panel_full = lax.all_gather(panel_strip, "col", axis=1, tiled=True)
    strip_all = lax.all_gather(panel_strip, "row", axis=0, tiled=True)
    column_full = lax.all_to_all(strip_all, "col", split_axis=0, concat_axis=1, tiled=True)
    pair = jnp.dot(
        panel_full,
        column_full.T,
        precision=lax.Precision.HIGHEST,
        preferred_element_type=jnp.float32,
    )
    partial_value = jnp.dot(
        coulomb * pair,
        column_full,
        precision=lax.Precision.HIGHEST,
        preferred_element_type=jnp.float32,
    )
    summed = lax.psum(partial_value, "col")
    weight_strip = lax.dynamic_slice_in_dim(summed, my_col * band_cols, band_cols, 1)
    weight_all = lax.all_gather(weight_strip, "row", axis=0, tiled=True)
    weight_column = lax.all_to_all(weight_all, "col", split_axis=0, concat_axis=1, tiled=True)
    term = -jnp.dot(
        fitting, weight_column, precision=lax.Precision.HIGHEST, preferred_element_type=jnp.float32
    )
    return lax.psum_scatter(term, "col", scatter_dimension=1, tiled=True)


def solution(mesh):
    in_specs = (P("row", "col"), P(), P("row", "col"), P("row", "col"))
    out_specs = P("row", "col")
    return jax.shard_map(
        per_device, mesh=mesh, in_specs=in_specs, out_specs=out_specs, check_vma=False
    )
```

profile of v0, /device:TPU:1, one launch (start us, length us, event | category | flops | bytes accessed | tf_op | source)
XLA Modules:
  0.0 455.0 jit_solution(17053227646644260959)
XLA Ops:
  6.5 0.0 copy-start
  6.5 0.9 add_select_fusion
  7.4 0.1 fusion.6
  7.5 18.1 %reduce-window.6 = s32[16,16,4,128]{3,1,2,0:T(8,128)S(1)} reduce-window(s32[16,16,4,128]{3,1,2,0:T(8,128)S(1)} %fusion.6, s32[]{:T(128)} %constant.16.clone.1), window={size=1x1x1x128 pad=0_0x0_0x0_0x127_0}, to_apply=%region_0.1 | reduce-window | flops 16646144 | bytes 1048580 | tf_op jit(solution)/shard_map/reduce-window
  25.6 0.2 slice.12
  25.9 0.4 copy.12
  26.3 0.1 fusion.8
  26.5 0.2 fusion.5
  26.7 0.4 fusion.3
  27.1 0.5 select_reduce_fusion
  27.7 0.1 reshape.84
  27.7 0.0 copy-done
  27.7 2.8 gather_fusion
  30.6 1.0 broadcast_select_fusion
  31.6 7.6 %all-to-all-start = ((f32[16,64,128]{2,1,0:T(8,128)}), f32[16,64,128]{2,1,0:T(8,128)S(1)}, u32[]{:S(2)}, u32[]{:S(2)}) async-start(f32[16,64,128]{2,1,0:T(8,128)} %broadcast_select_fusion), calls=%async_computation | async-start | bytes 1048576 | tf_op jit(solution)/shard_map/all_to_all | solution.py:28
  39.1 0.0 all-gather.10.cloned.1.call-start
  39.2 10.3 %all-to-all-done = f32[16,64,128]{2,1,0:T(8,128)S(1)} async-done(((f32[16,64,128]{2,1,0:T(8,128)}), f32[16,64,128]{2,1,0:T(8,128)S(1)}, u32[]{:S(2)}, u32[]{:S(2)}) %all-to-all-start) | async-done | bytes 524320 | tf_op jit(solution)/shard_map/all_to_all | solution.py:28
  49.6 1.6 gather_fusion.1
  51.2 0.0 all-gather.10.cloned.1.call-update
  51.2 0.0 all-gather.8.cloned.1.call-start
  51.3 0.7 all-gather.8.cloned.1.call-update
  52.0 50.4 %all-gather.10.cloned.1.call-done = f32[8192,128]{1,0:T(8,128)} async-done(((f32[512,128]{1,0:T(8,128)}), f32[8192,128]{1,0:T(8,128)}) %all-gather.10.cloned.1.call-update) | async-done | bytes 4194320 | tf_op jit(solution)/shard_map/all_gather | solution.py:34
  102.4 5.4 %copy.15 = f32[8,1024,128]{1,2,0:T(8,128)} copy(f32[8,1024,128]{2,1,0:T(8,128)} %bitcast.44) | data formatting | bytes 8388608 | tf_op jit(solution)/shard_map/all_to_all | solution.py:35
  107.7 5.3 %all-to-all-start.1 = ((f32[8,1024,128]{1,2,0:T(8,128)}), f32[8,1024,128]{1,2,0:T(8,128)}, u32[]{:S(2)}, u32[]{:S(2)}) async-start(f32[8,1024,128]{1,2,0:T(8,128)} %copy.15), calls=%async_computation.1 | async-start | bytes 8388608 | tf_op jit(solution)/shard_map/all_to_all | solution.py:35
  113.0 0.0 all-reduce.2.cloned.1.call-start
  113.0 31.5 %all-gather.8.cloned.1.call-done = f32[512,1024]{1,0:T(8,128)} async-done(((f32[512,128]{1,0:T(8,128)}), f32[512,1024]{1,0:T(8,128)}) %all-gather.8.cloned.1.call-update) | async-done | bytes 2097168 | tf_op jit(solution)/shard_map/all_gather | solution.py:33
  144.5 25.7 %all-to-all-done.1 = f32[8,1024,128]{1,2,0:T(8,128)} async-done(((f32[8,1024,128]{1,2,0:T(8,128)}), f32[8,1024,128]{1,2,0:T(8,128)}, u32[]{:S(2)}, u32[]{:S(2)}) %all-to-all-start.1) | async-done | bytes 4194336 | tf_op jit(solution)/shard_map/all_to_all | solution.py:35
  170.2 0.0 copy-start.1
  170.2 9.8 %fusion.11 = f32[512,1024]{1,0:T(8,128)S(1)} fusion(f32[512,1024]{1,0:T(8,128)} %all-gather.8.cloned.1.call-done, f32[1024,1024]{0,1:T(8,128)} %bitcast.10), kind=kOutput, calls=%fused_computation.34 | convolution fusion | flops 6442450944 | bytes 8388608 | tf_op jit(solution)/shard_map/dot_general | solution.py:36
  180.0 0.0 copy-done.1
  180.0 9.8 %fusion = f32[512,1024]{1,0:T(8,128)} fusion(f32[1024,1024]{0,1:T(8,128)} %bitcast.10, f32[512,1024]{1,0:T(8,128)S(1)} %copy-done.1, f32[512,1024]{1,0:T(8,128)S(1)} %fusion.11), kind=kOutput, calls=%fused_computation.3 | convolution fusion | flops 6442975232 | bytes 10485760 | tf_op jit(solution)/shard_map/dot_general | solution.py:42
  189.8 0.0 all-reduce.2.cloned.1.call-update
  189.8 0.0 all-gather.6.cloned.1.call-start
  189.9 62.2 %all-reduce.2.cloned.1.call-done = f32[512,1024]{1,0:T(8,128)} async-done(((f32[512,1024]{1,0:T(8,128)}), f32[512,1024]{1,0:T(8,128)}) %all-reduce.2.cloned.1.call-update) | async-done | bytes 2097168 | tf_op jit(solution)/shard_map/psum | solution.py:48
  252.1 1.7 constant_dynamic-slice_fusion
  253.7 0.0 all-gather.6.cloned.1.call-update
  253.7 0.0 reduce-scatter.2.cloned.1.call-start
  253.8 52.7 %all-gather.6.cloned.1.call-done = f32[8192,128]{1,0:T(8,128)} async-done(((f32[512,128]{1,0:T(8,128)}), f32[8192,128]{1,0:T(8,128)}) %all-gather.6.cloned.1.call-update) | async-done | bytes 4194320 | tf_op jit(solution)/shard_map/all_gather | solution.py:50
  306.5 5.4 %copy.16 = f32[8,1024,128]{1,2,0:T(8,128)} copy(f32[8,1024,128]{2,1,0:T(8,128)} %bitcast.45) | data formatting | bytes 8388608 | tf_op jit(solution)/shard_map/all_to_all | solution.py:51
  311.9 53.9 %all_to_all.43 = f32[8,1024,128]{1,2,0:T(8,128)S(1)} all-to-all(f32[8,1024,128]{1,2,0:T(8,128)} %copy.16), channel_id=1, replica_groups=mesh['row'=16,'col'=8] {'col'}, dimensions={0} | all-to-all | bytes 8388608 | tf_op jit(solution)/shard_map/all_to_all | solution.py:51
  365.8 29.9 %negate_bitcast_fusion = f32[2048,1024]{0,1:T(8,128)} fusion(f32[1024,1024]{0,1:T(8,128)S(1)} %bitcast.46, f32[2048,1024]{1,0:T(8,128)} %param.7), kind=kOutput, calls=%fused_computation.2 | convolution fusion | flops 25771900928 | bytes 20971520 | tf_op jit(solution)/shard_map/dot_general | solution.py:52
  395.6 0.0 reduce-scatter.2.cloned.1.call-update
  395.7 50.2 %reduce-scatter.2.cloned.1.call-done = f32[2048,128]{0,1:T(8,128)} async-done(((f32[2048,1024]{0,1:T(8,128)}), f32[2048,128]{0,1:T(8,128)}) %reduce-scatter.2.cloned.1.call-update) | async-done | bytes 1048592 | tf_op jit(solution)/shard_map/reduce_scatter | solution.py:55
  445.9 2.5 copy.17
  (9 shorter events, 0.1 us)
Async XLA Ops:
  6.5 21.2 %copy-start = (f32[2048,128]{1,0:T(8,128)S(1)}, f32[2048,128]{1,0:T(8,128)}, u32[]{:S(2)}) copy-start(f32[2048,128]{1,0:T(8,128)} %param.4) | copy-start | bytes 3145732
  31.6 18.0 %all-to-all-start = ((f32[16,64,128]{2,1,0:T(8,128)}), f32[16,64,128]{2,1,0:T(8,128)S(1)}, u32[]{:S(2)}, u32[]{:S(2)}) async-start(f32[16,64,128]{2,1,0:T(8,128)} %broadcast_select_fusion), calls=%async_computation | async-start | bytes 1048576 | tf_op jit(solution)/shard_map/all_to_all | solution.py:28
  39.1 63.2 %all-gather.10.cloned.1.call-start = ((), (), s32[]{:S(2)}) async-start(), calls=%async_computation.8 | async-start | bytes 4456448 | tf_op jit(solution)/shard_map/all_gather | solution.py:34
  51.2 93.3 %all-gather.8.cloned.1.call-start = ((), (), s32[]{:S(2)}) async-start(), calls=%async_computation.7 | async-start | bytes 2359296 | tf_op jit(solution)/shard_map/all_gather | solution.py:33
  107.7 62.5 %all-to-all-start.1 = ((f32[8,1024,128]{1,2,0:T(8,128)}), f32[8,1024,128]{1,2,0:T(8,128)}, u32[]{:S(2)}, u32[]{:S(2)}) async-start(f32[8,1024,128]{1,2,0:T(8,128)} %copy.15), calls=%async_computation.1 | async-start | bytes 8388608 | tf_op jit(solution)/shard_map/all_to_all | solution.py:35
  113.0 139.1 %all-reduce.2.cloned.1.call-start = ((), (), s32[]{:S(2)}) async-start(), calls=%async_computation.4 | async-start | bytes 4194304 | tf_op jit(solution)/shard_map/psum | solution.py:48
  170.2 9.8 %copy-start.1 = (f32[512,1024]{1,0:T(8,128)S(1)}, f32[512,1024]{1,0:T(8,128)}, u32[]{:S(2)}) copy-start(f32[512,1024]{1,0:T(8,128)} %param.6) | copy-start | bytes 6291460
  189.8 116.7 %all-gather.6.cloned.1.call-start = ((), (), s32[]{:S(2)}) async-start(), calls=%async_computation.5 | async-start | bytes 4456448 | tf_op jit(solution)/shard_map/all_gather | solution.py:50
  253.7 192.2 %reduce-scatter.2.cloned.1.call-start = ((), (), s32[]{:S(2)}) async-start(), calls=%async_computation.6 | async-start | bytes 9437184 | tf_op jit(solution)/shard_map/reduce_scatter | solution.py:55
Sparse Core Ops, SparseCore 0:
  51.3 50.9 all-gather.9
  104.0 40.3 all-gather.7
  190.0 62.0 all-reduce.1
  254.1 52.4 all-gather.5
  395.8 50.0 reduce-scatter.1
where the time goes:
time: 456 us; the launch traced here: 455 us
  waiting for transfers between devices  284 us (62%)
  blocking collectives  53.9 us (12%)
  matrix products  49.4 us (11%)
  other arithmetic  21.4 us (5%)
  local copies, waits for them, and re-layouts  20.1 us (4%)
  between operations  13.3 us (3%)
  starting transfers between devices  13 us (3%)
    psum x1, waiting for transfers between devices, per_device(): summed = lax.psum(partial_value, 'col')  62.2 us
    all_to_all x1, blocking collectives, per_device(): lax.all_to_all(weight_all, 'col', split_axis=0, concat_axis=1, tiled=True)  53.9 us
    all_gather x1, waiting for transfers between devices, per_device(): weight_all = lax.all_gather(weight_strip, 'row', axis=0, tiled=True)  52.7 us
    all_gather x1, waiting for transfers between devices, per_device(): strip_all = lax.all_gather(panel_strip, 'row', axis=0, tiled=True)  50.4 us
    reduce_scatter x1, waiting for transfers between devices, per_device(): return lax.psum_scatter(term, 'col', scatter_dimension=1, tiled=True)  50.2 us
    all_gather x1, waiting for transfers between devices, per_device(): panel_full = lax.all_gather(panel_strip, 'col', axis=1, tiled=True)  31.5 us
    dot_general x1, matrix products, per_device(): jnp.dot(fitting, weight_column, precision=lax.Precision.HIGHEST, preferre...  29.9 us
    all_to_all x1, waiting for transfers between devices, per_device(): lax.all_to_all(strip_all, 'col', split_axis=0, concat_axis=1, tiled=True)  25.7 us
  transfers between devices with their start and end apart: 7, of which 7 were waited for; matrix products, arithmetic and copies ran while one was open for 1% of the time, Pallas kernels for 0%

commit v1 on v0

--- a/solution.py
+++ b/solution.py
@@ -2,9 +2,14 @@
 import jax.numpy as jnp
 from jax import lax
 from jax.sharding import PartitionSpec as P
+from jax.lax import all_gather
 
 
 def per_device(orbitals, point_index, coulomb, fitting):
+
+    def put_columns(w_in):
+        return all_gather(w_in, axis_name="col").sum(axis=0)
+
     row_count = lax.axis_size("row")
     slab_rows = orbitals.shape[0]
     band_cols = orbitals.shape[1]
@@ -45,7 +50,7 @@
         precision=lax.Precision.HIGHEST,
         preferred_element_type=jnp.float32,
     )
-    summed = lax.psum(partial_value, "col")
+    summed = put_columns(partial_value)
     weight_strip = lax.dynamic_slice_in_dim(summed, my_col * band_cols, band_cols, 1)
     weight_all = lax.all_gather(weight_strip, "row", axis=0, tiled=True)
     weight_column = lax.all_to_all(weight_all, "col", split_axis=0, concat_axis=1, tiled=True)

time: 456 us -> 484 us (1.061)
  waiting for transfers between devices: 284 us -> 304 us
  other arithmetic: 21.4 us -> 29.3 us
    all_gather x0 -> x1, waiting for transfers between devices: none -> 83.6 us  [put_columns(): return all_gather(w_in, axis_name='col').sum(axis=0)]
    psum x1 -> x0, waiting for transfers between devices: 62.2 us -> none  [per_device(): summed = lax.psum(partial_value, 'col')]
    reduce_sum x0 -> x1, other arithmetic: none -> 7.96 us  [put_columns(): return all_gather(w_in, axis_name='col').sum(axis=0)]
where the time goes in v1:
time: 484 us; the launch traced here: 483 us
  waiting for transfers between devices  304 us (63%)
  blocking collectives  54.2 us (11%)
  matrix products  50.6 us (10%)
  other arithmetic  29.3 us (6%)
  local copies, waits for them, and re-layouts  19.2 us (4%)
  between operations  13.3 us (3%)
  starting transfers between devices  13 us (3%)
    all_gather x1, waiting for transfers between devices, put_columns(): return all_gather(w_in, axis_name='col').sum(axis=0)  83.6 us
    all_to_all x1, blocking collectives, per_device(): lax.all_to_all(weight_all, 'col', split_axis=0, concat_axis=1, tiled=True)  54.2 us
    all_gather x1, waiting for transfers between devices, per_device(): weight_all = lax.all_gather(weight_strip, 'row', axis=0, tiled=True)  51.2 us
    all_gather x1, waiting for transfers between devices, per_device(): strip_all = lax.all_gather(panel_strip, 'row', axis=0, tiled=True)  50.4 us
    reduce_scatter x1, waiting for transfers between devices, per_device(): return lax.psum_scatter(term, 'col', scatter_dimension=1, tiled=True)  50.2 us
    all_gather x1, waiting for transfers between devices, per_device(): panel_full = lax.all_gather(panel_strip, 'col', axis=1, tiled=True)  31.5 us
    dot_general x1, matrix products, per_device(): jnp.dot(fitting, weight_column, precision=lax.Precision.HIGHEST, preferre...  31 us
    all_to_all x1, waiting for transfers between devices, per_device(): lax.all_to_all(strip_all, 'col', split_axis=0, concat_axis=1, tiled=True)  25.7 us
  transfers between devices with their start and end apart: 7, of which 7 were waited for; matrix products, arithmetic and copies ran while one was open for 1% of the time, Pallas kernels for 0%

profile of v1, /device:TPU:1, one launch (start us, length us, event | category | flops | bytes accessed | tf_op | source)
XLA Modules:
  0.0 483.5 jit_solution(137309192027345048)
XLA Ops:
  6.5 0.0 copy-start
  6.5 0.9 add_select_fusion
  7.4 0.1 fusion.6
  7.5 18.1 %reduce-window.6 = s32[16,16,4,128]{3,1,2,0:T(8,128)S(1)} reduce-window(s32[16,16,4,128]{3,1,2,0:T(8,128)S(1)} %fusion.6, s32[]{:T(128)} %constant.16.clone.1), window={size=1x1x1x128 pad=0_0x0_0x0_0x127_0}, to_apply=%region_0.1 | reduce-window | flops 16646144 | bytes 1048580 | tf_op jit(solution)/shard_map/reduce-window
  25.6 0.2 slice.12
  25.9 0.4 copy.17
  26.3 0.1 fusion.8
  26.5 0.2 fusion.5
  26.7 0.4 fusion.3
  27.1 0.5 select_reduce_fusion
  27.7 0.1 reshape.84
  27.7 0.0 copy-done
  27.7 2.8 gather_fusion
  30.6 1.0 broadcast_select_fusion
  31.6 7.6 %all-to-all-start = ((f32[16,64,128]{2,1,0:T(8,128)}), f32[16,64,128]{2,1,0:T(8,128)S(1)}, u32[]{:S(2)}, u32[]{:S(2)}) async-start(f32[16,64,128]{2,1,0:T(8,128)} %broadcast_select_fusion), calls=%async_computation | async-start | bytes 1048576 | tf_op jit(solution)/shard_map/all_to_all | solution.py:33
  39.1 0.0 all-gather.12.cloned.1.call-start
  39.2 10.3 %all-to-all-done = f32[16,64,128]{2,1,0:T(8,128)S(1)} async-done(((f32[16,64,128]{2,1,0:T(8,128)}), f32[16,64,128]{2,1,0:T(8,128)S(1)}, u32[]{:S(2)}, u32[]{:S(2)}) %all-to-all-start) | async-done | bytes 524320 | tf_op jit(solution)/shard_map/all_to_all | solution.py:33
  49.6 1.6 gather_fusion.1
  51.2 0.0 all-gather.12.cloned.1.call-update
  51.2 0.0 all-gather.10.cloned.1.call-start
  51.3 0.7 all-gather.10.cloned.1.call-update
  52.0 50.4 %all-gather.12.cloned.1.call-done = f32[8192,128]{1,0:T(8,128)} async-done(((f32[512,128]{1,0:T(8,128)}), f32[8192,128]{1,0:T(8,128)}) %all-gather.12.cloned.1.call-update) | async-done | bytes 4194320 | tf_op jit(solution)/shard_map/all_gather | solution.py:39
  102.4 5.4 %copy.20 = f32[8,1024,128]{1,2,0:T(8,128)} copy(f32[8,1024,128]{2,1,0:T(8,128)} %bitcast.46) | data formatting | bytes 8388608 | tf_op jit(solution)/shard_map/all_to_all | solution.py:40
  107.7 5.3 %all-to-all-start.1 = ((f32[8,1024,128]{1,2,0:T(8,128)}), f32[8,1024,128]{1,2,0:T(8,128)}, u32[]{:S(2)}, u32[]{:S(2)}) async-start(f32[8,1024,128]{1,2,0:T(8,128)} %copy.20), calls=%async_computation.1 | async-start | bytes 8388608 | tf_op jit(solution)/shard_map/all_to_all | solution.py:40
  113.0 0.0 all-gather.14.cloned.1.call-start
  113.0 31.5 %all-gather.10.cloned.1.call-done = f32[512,1024]{1,0:T(8,128)} async-done(((f32[512,128]{1,0:T(8,128)}), f32[512,1024]{1,0:T(8,128)}) %all-gather.10.cloned.1.call-update) | async-done | bytes 2097168 | tf_op jit(solution)/shard_map/all_gather | solution.py:38
  144.5 25.7 %all-to-all-done.1 = f32[8,1024,128]{1,2,0:T(8,128)} async-done(((f32[8,1024,128]{1,2,0:T(8,128)}), f32[8,1024,128]{1,2,0:T(8,128)}, u32[]{:S(2)}, u32[]{:S(2)}) %all-to-all-start.1) | async-done | bytes 4194336 | tf_op jit(solution)/shard_map/all_to_all | solution.py:40
  170.2 0.0 copy-start.2
  170.2 9.8 %fusion.11 = f32[512,1024]{1,0:T(8,128)S(1)} fusion(f32[512,1024]{1,0:T(8,128)} %all-gather.10.cloned.1.call-done, f32[1024,1024]{0,1:T(8,128)} %bitcast.10), kind=kOutput, calls=%fused_computation.34 | convolution fusion | flops 6442450944 | bytes 8388608 | tf_op jit(solution)/shard_map/dot_general | solution.py:41
  180.0 0.0 copy-done.2
  180.0 9.8 %fusion = f32[512,1024]{1,0:T(8,128)} fusion(f32[1024,1024]{0,1:T(8,128)} %bitcast.10, f32[512,1024]{1,0:T(8,128)S(1)} %copy-done.2, f32[512,1024]{1,0:T(8,128)S(1)} %fusion.11), kind=kOutput, calls=%fused_computation.3 | convolution fusion | flops 6442975232 | bytes 10485760 | tf_op jit(solution)/shard_map/dot_general | solution.py:47
  189.8 0.0 all-gather.14.cloned.1.call-update
  189.9 0.0 all-gather.8.cloned.1.call-start
  189.9 83.6 %all-gather.14.cloned.1.call-done = f32[4096,1024]{1,0:T(8,128)} async-done(((f32[512,1024]{1,0:T(8,128)}), f32[4096,1024]{1,0:T(8,128)}) %all-gather.14.cloned.1.call-update) | async-done | bytes 16777232 | tf_op jit(solution)/shard_map/all_gather | solution.py:11
  273.6 8.0 %reduce_sum.32 = f32[512,1024]{1,0:T(8,128)S(1)} reduce(f32[8,512,1024]{2,1,0:T(8,128)} %bitcast.43, f32[]{:T(128)} %constant.44.clone.1), dimensions={0}, to_apply=%region_5.6 | reduce | flops 3670016 | bytes 18874372 | tf_op jit(solution)/shard_map/reduce_sum | solution.py:11
  281.5 0.7 constant_dynamic-slice_fusion
  282.3 0.0 all-gather.8.cloned.1.call-update
  282.3 0.0 reduce-scatter.2.cloned.1.call-start
  282.4 51.2 %all-gather.8.cloned.1.call-done = f32[8192,128]{1,0:T(8,128)} async-done(((f32[512,128]{1,0:T(8,128)}), f32[8192,128]{1,0:T(8,128)}) %all-gather.8.cloned.1.call-update) | async-done | bytes 4194320 | tf_op jit(solution)/shard_map/all_gather | solution.py:55
  333.6 54.2 %all_to_all.43 = f32[8,1024,128]{2,1,0:T(8,128)} all-to-all(f32[8,1024,128]{2,1,0:T(8,128)} %bitcast.47), channel_id=1, replica_groups=mesh['row'=16,'col'=8] {'col'}, dimensions={0} | all-to-all | bytes 8388608 | tf_op jit(solution)/shard_map/all_to_all | solution.py:56
  387.8 5.3 %copy.21 = f32[1024,8,128]{0,2,1:T(8,128)} copy(f32[1024,8,128]{2,0,1:T(8,128)} %bitcast.44) | data formatting | bytes 8388608 | tf_op jit(solution)/shard_map/all_to_all | solution.py:56
  393.1 31.0 %negate_bitcast_fusion = f32[2048,1024]{0,1:T(8,128)} fusion(f32[1024,1024]{0,1:T(8,128)} %bitcast.48, f32[2048,1024]{1,0:T(8,128)} %param.7), kind=kOutput, calls=%fused_computation.2 | convolution fusion | flops 25771900928 | bytes 20971520 | tf_op jit(solution)/shard_map/dot_general | solution.py:57
  424.2 0.0 reduce-scatter.2.cloned.1.call-update
  424.2 0.0 copy-start.1
  424.2 50.2 %reduce-scatter.2.cloned.1.call-done = f32[2048,128]{0,1:T(8,128)} async-done(((f32[2048,1024]{0,1:T(8,128)}), f32[2048,128]{0,1:T(8,128)}) %reduce-scatter.2.cloned.1.call-update) | async-done | bytes 1048592 | tf_op jit(solution)/shard_map/reduce_scatter | solution.py:60
  474.4 2.5 copy.22
  477.0 0.0 copy-done.1
  (9 shorter events, 0.1 us)
Async XLA Ops:
  6.5 21.2 %copy-start = (f32[2048,128]{1,0:T(8,128)S(1)}, f32[2048,128]{1,0:T(8,128)}, u32[]{:S(2)}) copy-start(f32[2048,128]{1,0:T(8,128)} %param.4) | copy-start | bytes 3145732
  31.6 18.0 %all-to-all-start = ((f32[16,64,128]{2,1,0:T(8,128)}), f32[16,64,128]{2,1,0:T(8,128)S(1)}, u32[]{:S(2)}, u32[]{:S(2)}) async-start(f32[16,64,128]{2,1,0:T(8,128)} %broadcast_select_fusion), calls=%async_computation | async-start | bytes 1048576 | tf_op jit(solution)/shard_map/all_to_all | solution.py:33
  39.1 63.2 %all-gather.12.cloned.1.call-start = ((), (), s32[]{:S(2)}) async-start(), calls=%async_computation.7 | async-start | bytes 4456448 | tf_op jit(solution)/shard_map/all_gather | solution.py:39
  51.2 93.3 %all-gather.10.cloned.1.call-start = ((), (), s32[]{:S(2)}) async-start(), calls=%async_computation.6 | async-start | bytes 2359296 | tf_op jit(solution)/shard_map/all_gather | solution.py:38
  107.7 62.5 %all-to-all-start.1 = ((f32[8,1024,128]{1,2,0:T(8,128)}), f32[8,1024,128]{1,2,0:T(8,128)}, u32[]{:S(2)}, u32[]{:S(2)}) async-start(f32[8,1024,128]{1,2,0:T(8,128)} %copy.20), calls=%async_computation.1 | async-start | bytes 8388608 | tf_op jit(solution)/shard_map/all_to_all | solution.py:40
  113.0 160.6 %all-gather.14.cloned.1.call-start = ((), (), s32[]{:S(2)}) async-start(), calls=%async_computation.8 | async-start | bytes 18874368 | tf_op jit(solution)/shard_map/all_gather | solution.py:11
  170.2 9.8 %copy-start.2 = (f32[512,1024]{1,0:T(8,128)S(1)}, f32[512,1024]{1,0:T(8,128)}, u32[]{:S(2)}) copy-start(f32[512,1024]{1,0:T(8,128)} %param.6) | copy-start | bytes 6291460
  189.9 143.7 %all-gather.8.cloned.1.call-start = ((), (), s32[]{:S(2)}) async-start(), calls=%async_computation.4 | async-start | bytes 4456448 | tf_op jit(solution)/shard_map/all_gather | solution.py:55
  282.3 192.1 %reduce-scatter.2.cloned.1.call-start = ((), (), s32[]{:S(2)}) async-start(), calls=%async_computation.5 | async-start | bytes 9437184 | tf_op jit(solution)/shard_map/reduce_scatter | solution.py:60
  424.2 52.8 %copy-start.1 = (f32[2048,128]{1,0:T(8,128)S(1)}, f32[2048,128]{1,0:T(8,128)}, u32[]{:S(2)}) copy-start(f32[2048,128]{1,0:T(8,128)} %param.4) | copy-start | bytes 3145732
Sparse Core Ops, SparseCore 0:
  51.3 50.9 all-gather.11
  104.0 40.4 all-gather.9
  190.0 83.5 all-gather.13
  282.4 51.1 all-gather.7
  424.3 50.0 reduce-scatter.1
